TPU v7x, 128 devices: a whole 4x4x4 slice. The times are simulated.
128 devices in a mesh: grp: 4 (over y), col: 32 (over x, z, core).
Axes of the slice: x: 4, y: 4, z: 4, core: 2. Of those that a mesh axis runs over, the one named last changes fastest.
Arguments:
- blocks: bfloat16 [24576, 32, 1024], P(('grp', 'col'))
- i_index: int32 [24576], P(('grp', 'col')), may hold values from 0 to 63
- j_index: int32 [24576], P(('grp', 'col')), may hold values from 0 to 63
- k_index: int32 [24576], P(('grp', 'col')), may hold values from 0 to 15
- block_count: int32 [128], P(('grp', 'col')), may hold values from 24 to 192, as said below
- b_factor: float32 [65536, 256], P(('grp', 'col'))
- c_factor: float32 [16384, 256], P(('grp', 'col'))
Outputs:
- a_update: float32 [8192, 256], P(('grp', 'col'))
- b_update: float32 [65536, 256], P(('grp', 'col'))
Inputs may be any that keep to these rules, and one draw needn't show every extreme that they name: block_count[d] is the number of live slots of device d = 32 * (grp index) + (col index): its slots d * 192 to d * 192 + block_count[d] - 1; every other slot is ignored. Some device has exactly 192 live slots.
All inputs are finite; a program needn't handle non-finite values.
Results may differ from a plain program's by a relative error of at most 0.005.
The roundings to bfloat16 on the way count: a program that leaves them out, or rounds other values in their place, can miss the bound.
Values may be sent and summed in bfloat16 or wider, within the bound.
No kernel may reach another device: no remote copies, remote signals or barrier semaphores. Data moves between devices by JAX's collectives and lax.ppermute only.
A program may use at most 128 MiB of HBM per device.

v0:
```python
import jax
import jax.numpy as jnp
from jax import lax
from jax.sharding import PartitionSpec as P

A_DEV = 2


def solve_rows(gram, right_side):
    factor_low = lax.linalg.cholesky(gram)
    halfway = lax.linalg.triangular_solve(
        factor_low, right_side, left_side=False, lower=True, transpose_a=True
    )
    return lax.linalg.triangular_solve(
        factor_low, halfway, left_side=False, lower=True, transpose_a=False
    )


def mode_term(
    blocks,
    left_rows,
    left_index,
    tail_rows,
    tail_index,
    target_index,
    live_mask,
    targets,
    first_mode,
):
    block_edge = blocks.shape[1]
    rank_width = left_rows.shape[1]
    group_size = 16
    groups = blocks.shape[0] // group_size
    left_table = left_rows.reshape(-1, block_edge, rank_width)
    tail_table = tail_rows.reshape(-1, block_edge, rank_width)
    target_ids = jnp.arange(targets, dtype=jnp.int32)

    def one_step(running, inputs):
        tensor_group, left_idx, tail_idx, target_idx, alive_row = inputs
        left_blk = left_table[left_idx].astype(jnp.float32)
        tail_blk = tail_table[tail_idx].astype(jnp.float32)
        product = (left_blk[:, :, None, :] * tail_blk[:, None, :, :]).astype(jnp.bfloat16)
        if first_mode:
            result = jnp.einsum(
                "bim,bmr->bir",
                tensor_group,
                product.reshape(group_size, block_edge * block_edge, rank_width),
                preferred_element_type=jnp.float32,
            )
        else:
            result = jnp.einsum(
                "bijk,bikr->bjr",
                tensor_group.reshape(group_size, block_edge, block_edge, block_edge),
                product,
                preferred_element_type=jnp.float32,
            )
        select = (target_idx[None, :] == target_ids[:, None]).astype(jnp.float32) * alive_row[
            None, :
        ]
        update = jnp.dot(
            select,
            result.reshape(group_size, block_edge * rank_width),
            precision=lax.Precision.HIGHEST,
        )
        return (running + update, None)

    inputs = (
        blocks.reshape(groups, group_size, block_edge, block_edge * block_edge),
        left_index.reshape(groups, group_size),
        tail_index.reshape(groups, group_size),
        target_index.reshape(groups, group_size),
        live_mask.reshape(groups, group_size),
    )
    start_value = jnp.zeros((targets, block_edge * rank_width), jnp.float32)
    running, _ = lax.scan(one_step, start_value, inputs)
    return running.reshape(targets * block_edge, rank_width)


def on_device(blocks, i_index, j_index, k_index, block_count, b_factor, c_factor):
    highest = lax.Precision.HIGHEST
    block_edge = blocks.shape[1]
    gram_second, gram_third = lax.psum(
        (
            jnp.dot(b_factor.T, b_factor, precision=highest),
            jnp.dot(c_factor.T, c_factor, precision=highest),
        ),
        ("grp", "col"),
    )
    b_range, c_range = (
        lax.all_gather(b_factor.astype(jnp.bfloat16), "grp", axis=0, tiled=True),
        lax.all_gather(c_factor.astype(jnp.bfloat16), "grp", axis=0, tiled=True),
    )
    live_mask = (jnp.arange(blocks.shape[0], dtype=jnp.int32) < block_count[0]).astype(jnp.float32)
    first_targets = A_DEV * lax.axis_size("col")
    second_targets = b_range.shape[0] // block_edge
    partial_value = mode_term(
        blocks, b_range, j_index, c_range, k_index, i_index, live_mask, first_targets, True
    )
    gram_one = gram_second * gram_third
    whole_sum = lax.psum(partial_value, "col")
    a_whole = solve_rows(gram_one, whole_sum)
    gram_first = lax.psum(jnp.dot(a_whole.T, a_whole, precision=highest), "grp")
    col_norm = jnp.sqrt(jnp.diagonal(gram_first) + 1e-06)
    a_range = (a_whole / col_norm[None, :]).astype(jnp.bfloat16)
    own_rows = A_DEV * block_edge
    a_update = lax.dynamic_slice_in_dim(a_whole, lax.axis_index("col") * own_rows, own_rows, 0)
    gram_two = gram_first / (col_norm[:, None] * col_norm[None, :]) * gram_third
    partial_two = mode_term(
        blocks, a_range, i_index, c_range, k_index, j_index, live_mask, second_targets, False
    )
    own_two = lax.psum_scatter(partial_two, "grp", scatter_dimension=0, tiled=True)
    b_update = solve_rows(gram_two, own_two)
    return (a_update, b_update)


def solution(mesh):
    return jax.shard_map(
        on_device,
        mesh=mesh,
        in_specs=(
            P(("grp", "col"), None, None),
            P(("grp", "col")),
            P(("grp", "col")),
            P(("grp", "col")),
            P(("grp", "col")),
            P(("grp", "col"), None),
            P(("grp", "col"), None),
        ),
        out_specs=(P(("grp", "col"), None), P(("grp", "col"), None)),
        check_vma=False,
    )
```

profile of v0, /device:TPU:0, one launch (start us, length us, event | category | flops | bytes accessed | tf_op | source)
XLA Modules:
  0.0 780.1 jit_solution(10742429783290168959)
XLA Ops:
  8.1 2.9 fusion.61
  15.0 13.0 %all_gather.7 = bf16[512,256]{1,0:T(8,128)(2,1)S(1)} all-gather(bf16[128,256]{1,0:T(8,128)(2,1)S(1)} %convert_element_type.56), channel_id=1, replica_groups=mesh['grp'=4,'col'=32] {'grp'}, dimensions={0}, use_global_device_ids=true | all-gather | bytes 327680 | tf_op jit(solution)/shard_map/all_gather | solution.py:91
  28.0 135.6 %all-reduce.10.cloned.1.call-done = (f32[256,256]{0,1:T(8,128)}, f32[256,256]{0,1:T(8,128)}) async-done(((f32[256,256]{0,1:T(8,128)}, f32[256,256]{0,1:T(8,128)}), (f32[256,256]{0,1:T(8,128)}, f32[256,256]{0,1:T(8,128)})) %all-reduce.10.cloned.1.call-update) | async-done | bytes 524304 | tf_op jit(solution)/shard_map/psum | solution.py:82
  164.8 11.7 %custom-call.29 = f32[128,128]{1,0:T(8,128)S(1)} custom-call(f32[128,128]{1,0:T(8,128)S(1)} %slice.101), custom_call_target="Cholesky" | custom-call | tf_op jit(solution)/shard_map/cholesky/custom-call.2 | solution.py:10
  176.6 9.8 %custom-call.30 = f32[1,128,128]{1,2,0:T(8,128)S(1)} custom-call(f32[1,128,128]{2,1,0:T(8,128)S(1)} %get-tuple-element.262), custom_call_target="InvertDiagBlocksLowerTriangular" | custom-call | tf_op jit(solution)/shard_map/cholesky/custom-call.7 | solution.py:10
  187.1 11.7 %custom-call.31 = f32[128,128]{1,0:T(8,128)S(1)} custom-call(f32[128,128]{1,0:T(8,128)S(1)} %convolution_subtract_fusion.5), custom_call_target="Cholesky" | custom-call | tf_op jit(solution)/shard_map/cholesky/custom-call.3 | solution.py:10
  198.9 141.3 %while.26 = (s32[]{:T(128)}, f32[64,8192]{1,0:T(8,128)S(1)}, s32[12,16]{1,0:T(8,128)S(1)}, f32[12,16]{1,0:T(8,128)S(1)}, bf16[12,16,32,1024]{3,2,1,0:T(8,128)(2,...) while((s32[]{:T(128)}, f32[64,8192]{1,0:T(8,128)S(1)}, ...), condition=%wide.region_1.0_spmd.clone, body=%wide.region_0.0_spmd.clone.sunk | while | flops 378802272 | bytes 27796492 | solution.py:75
  201.6 3.9 multiply_convert_fusion.5
  205.4 2.7 fusion.109
  213.3 3.9 multiply_convert_fusion.5
  225.1 3.9 multiply_convert_fusion.5
  228.9 2.7 fusion.109
  236.8 3.9 multiply_convert_fusion.5
  240.7 2.7 fusion.109
  248.6 3.9 multiply_convert_fusion.5
  252.5 2.7 fusion.109
  260.4 3.9 multiply_convert_fusion.5
  264.2 2.7 fusion.109
  272.1 3.9 multiply_convert_fusion.5
  276.0 2.7 fusion.109
  283.9 3.9 multiply_convert_fusion.5
  287.8 2.7 fusion.109
  295.7 3.9 multiply_convert_fusion.5
  299.5 2.7 fusion.109
  307.4 3.9 multiply_convert_fusion.5
  311.3 2.7 fusion.109
  319.2 3.9 multiply_convert_fusion.5
  323.1 2.7 fusion.109
  331.0 3.9 multiply_convert_fusion.5
  344.0 4.3 while.24
  348.3 19.7 %custom-call.20 = f32[2,128,128]{1,2,0:T(8,128)S(1)} custom-call(f32[2,128,128]{2,1,0:T(8,128)S(1)} %get-tuple-element.116), custom_call_target="InvertDiagBlocksLowerTriangular" | custom-call | tf_op jit(solution)/shard_map/triangular_solve | solution.py:11
  368.0 80.2 %all-reduce.6.cloned.1.call-done = f32[2048,256]{1,0:T(8,128)} async-done(((f32[2048,256]{1,0:T(8,128)}), f32[2048,256]{1,0:T(8,128)}) %all-reduce.6.cloned.1.call-update) | async-done | bytes 2097168 | tf_op jit(solution)/shard_map/psum | solution.py:100
  456.5 4.2 fusion.33
  461.2 40.8 %all-reduce.8.cloned.1.call-done = f32[256,256]{0,1:T(8,128)} async-done(((f32[256,256]{0,1:T(8,128)}), f32[256,256]{0,1:T(8,128)}) %all-reduce.8.cloned.1.call-update) | async-done | bytes 262160 | tf_op jit(solution)/shard_map/psum | solution.py:102
  507.1 195.0 %while.27 = (s32[]{:T(128)}, f32[64,8192]{1,0:T(8,128)S(1)}, s32[12,16]{1,0:T(8,128)}, f32[12,16]{1,0:T(8,128)}, bf16[12,16,32,1024]{3,2,1,0:T(8,128)(2,1)}, /*i...) while((s32[]{:T(128)}, f32[64,8192]{1,0:T(8,128)S(1)}, ...), condition=%wide.region_11.13_spmd.clone, body=%wide.region_10.12_spmd.clone.sunk | while | flops 378802272 | bytes 15213583 | solution.py:75
  508.4 4.4 reshape.345
  515.3 4.0 fusion.116
  524.7 4.4 reshape.345
  531.5 4.0 fusion.116
  540.9 4.4 reshape.345
  547.8 4.0 fusion.116
  557.2 4.4 reshape.345
  564.0 4.0 fusion.116
  573.4 4.4 reshape.345
  580.3 4.0 fusion.116
  589.7 4.4 reshape.345
  596.5 4.0 fusion.116
  605.9 4.4 reshape.345
  612.8 4.0 fusion.116
  622.2 4.4 reshape.345
  629.0 4.0 fusion.116
  638.4 4.4 reshape.345
  645.3 4.0 fusion.116
  654.7 4.4 reshape.345
  661.5 4.0 fusion.116
  670.9 4.4 reshape.345
  677.8 4.0 fusion.116
  687.2 4.4 reshape.345
  694.0 4.0 fusion.116
  706.2 11.7 %custom-call.32 = f32[128,128]{1,0:T(8,128)S(1)} custom-call(f32[128,128]{1,0:T(8,128)S(1)} %slice.104), custom_call_target="Cholesky" | custom-call | tf_op jit(solution)/shard_map/cholesky/custom-call.2 | solution.py:10
  718.0 9.8 %custom-call.33 = f32[1,128,128]{1,2,0:T(8,128)S(1)} custom-call(f32[1,128,128]{2,1,0:T(8,128)S(1)} %get-tuple-element.258), custom_call_target="InvertDiagBlocksLowerTriangular" | custom-call | tf_op jit(solution)/shard_map/cholesky/custom-call.7 | solution.py:10
  728.5 11.7 %custom-call.34 = f32[128,128]{1,0:T(8,128)S(1)} custom-call(f32[128,128]{1,0:T(8,128)S(1)} %convolution_subtract_fusion.4), custom_call_target="Cholesky" | custom-call | tf_op jit(solution)/shard_map/cholesky/custom-call.3 | solution.py:10
  742.9 4.0 while.25
  746.9 19.8 %custom-call.21 = f32[2,128,128]{1,2,0:T(8,128)S(1)} custom-call(f32[2,128,128]{2,1,0:T(8,128)S(1)} %get-tuple-element.124), custom_call_target="InvertDiagBlocksLowerTriangular" | custom-call | tf_op jit(solution)/shard_map/triangular_solve | solution.py:11
  (399 shorter events, 200.5 us)
Async XLA Ops:
  8.0 5.2 copy-start.5
  8.0 6.0 copy-start.8
  8.0 6.0 copy-start.12
  8.0 6.8 copy-start.13
  8.0 6.9 copy-start.14
  8.0 155.5 %all-reduce.10.cloned.1.call-start = ((), (), s32[]{:S(2)}) async-start(), calls=%async_computation.5 | async-start | bytes 1048576 | tf_op jit(solution)/shard_map/psum | solution.py:82
  13.2 185.7 %all-gather.2.cloned.1.call-start = ((), (), s32[]{:S(2)}) async-start(), calls=%async_computation.1 | async-start | bytes 1310720 | tf_op jit(solution)/shard_map/all_gather | solution.py:90
  14.0 434.3 %all-reduce.6.cloned.1.call-start = ((), (), s32[]{:S(2)}) async-start(), calls=%async_computation.2 | async-start | bytes 4194304 | tf_op jit(solution)/shard_map/psum | solution.py:100
  340.2 1.5 copy-start.10
  340.2 1.5 copy-start.11
  341.8 160.2 %all-reduce.8.cloned.1.call-start = ((), (), s32[]{:S(2)}) async-start(), calls=%async_computation.3 | async-start | bytes 524288 | tf_op jit(solution)/shard_map/psum | solution.py:102
  348.3 103.3 %copy-start.7 = (f32[256,256]{1,0:T(8,128)}, f32[256,256]{1,0:T(8,128)S(1)}, u32[]{:S(2)}) copy-start(f32[256,256]{1,0:T(8,128)S(1)} %get-tuple-element.553) | copy-start | bytes 786436
  348.3 103.3 %copy-start.15 = (s32[2,2]{1,0:T(2,128)}, s32[2,2]{1,0:T(2,128)S(1)}, u32[]{:S(2)}) copy-start(s32[2,2]{1,0:T(2,128)S(1)} %get-tuple-element.571) | copy-start | bytes 52
  448.3 2.4 copy-start.6
  453.6 51.0 %copy-start = (f32[2048,128]{1,0:T(8,128)}, f32[2048,128]{1,0:T(8,128)S(1)}, u32[]{:S(2)}) copy-start(f32[2048,128]{1,0:T(8,128)S(1)} %fusion.48) | copy-start | bytes 3145732
  456.5 4.7 copy-start.2
  460.7 306.1 %reduce-scatter.2.cloned.1.call-start = ((), (), s32[]{:S(2)}) async-start(), calls=%async_computation.4 | async-start | bytes 2621440 | tf_op jit(solution)/shard_map/reduce_scatter | solution.py:111
  703.6 1.2 copy-start.1
  703.6 1.5 copy-start.3
  703.6 2.2 copy-start.4
  703.6 2.2 copy-start.9
  706.0 36.9 %copy-start.16 = (s32[2,2]{1,0:T(2,128)S(1)}, s32[2,2]{1,0:T(2,128)}, u32[]{:S(2)}) copy-start(s32[2,2]{1,0:T(2,128)} %copy-done.15) | copy-start | bytes 52
Sparse Core Ops, SparseCore 0:
  13.8 149.6 all-reduce.9
Sparse Core Ops, SparseCore 1:
  15.9 26.6 all-gather.1
  341.9 106.3 all-reduce.5
  460.8 41.2 all-reduce.7
  703.7 30.0 reduce-scatter.1
where the time goes:
time: 792 us; the launch traced here: 780 us
  waiting for transfers between devices  257 us (32%)
  local copies, waits for them, and re-layouts  166 us (21%)
  other arithmetic  162 us (20%)
  matrix products  159 us (20%)
  between operations  19.7 us (2%)
  blocking collectives  13 us (2%)
    psum x1, waiting for transfers between devices, on_device(): lax.psum((jnp.dot(b_factor.T, b_factor, precision=highest), jnp.dot(c_fac...  136 us
    psum x1, waiting for transfers between devices, on_device(): whole_sum = lax.psum(partial_value, 'col')  80.2 us
    another operation x13, other arithmetic, solve_rows(): factor_low = lax.linalg.cholesky(gram)  68.6 us
    dot_general x24, matrix products, one_step(): jnp.dot(select, result.reshape(group_size, block_edge * rank_width), prec...  55 us
    reshape x12, local copies, waits for them, and re-layouts, one_step(): tensor_group.reshape(group_size, block_edge, block_edge, block_edge)  52.3 us
    dot_general x12, matrix products, one_step(): jnp.einsum('bijk,bikr->bjr', tensor_group.reshape(group_size, block_edge,...  48.5 us
    convert_element_type x12, other arithmetic, one_step(): (left_blk[:, :, None, :] * tail_blk[:, None, :, :]).astype(jnp.bfloat16)  46.2 us
    gather x24, local copies, waits for them, and re-layouts, one_step(): left_blk = left_table[left_idx].astype(jnp.float32)  42.9 us
  transfers between devices with their start and end apart: 5, of which 3 were waited for; matrix products, arithmetic and copies ran while one was open for 15% of the time, Pallas kernels for 0%

commit v1 on v0

--- a/solution.py
+++ b/solution.py
@@ -97,7 +97,7 @@
         blocks, b_range, j_index, c_range, k_index, i_index, live_mask, first_targets, True
     )
     gram_one = gram_second * gram_third
-    whole_sum = lax.psum(partial_value, "col")
+    whole_sum = jnp.sum(lax.all_gather(partial_value, "col"), axis=0)
     a_whole = solve_rows(gram_one, whole_sum)
     gram_first = lax.psum(jnp.dot(a_whole.T, a_whole, precision=highest), "grp")
     col_norm = jnp.sqrt(jnp.diagonal(gram_first) + 1e-06)

time: 792 us -> 742 us (0.937)
  waiting for transfers between devices: 257 us -> 191 us
  other arithmetic: 162 us -> 184 us
    all_gather x0 -> x1, waiting for transfers between devices: none -> 140 us  [on_device(): whole_sum = jnp.sum(lax.all_gather(partial_value, 'col'), axis=0)]
    psum x1, waiting for transfers between devices: 136 us -> 0.03 us  [on_device(): lax.psum((jnp.dot(b_factor.T, b_factor, precision=highest), jnp.dot(c_fac...]
    psum x1 -> x0, waiting for transfers between devices: 80.2 us -> none  [on_device(): whole_sum = lax.psum(partial_value, 'col')]
    reduce_sum x0 -> x1, other arithmetic: none -> 21.2 us  [on_device(): whole_sum = jnp.sum(lax.all_gather(partial_value, 'col'), axis=0)]
    all_gather x1, waiting for transfers between devices: 0.03 us -> 9.78 us  [on_device(): lax.all_gather(b_factor.astype(jnp.bfloat16), 'grp', axis=0, tiled=True)]
  transfers between devices with their start and end apart: 5 -> 5, of which waited for: 3 -> 3; matrix products, arithmetic and copies ran while one was open for 15% -> 36% of each run, Pallas kernels for 0% -> 0%
where the time goes in v1:
time: 742 us; the launch traced here: 733 us
  waiting for transfers between devices  191 us (26%)
  other arithmetic  184 us (25%)
  local copies, waits for them, and re-layouts  166 us (22%)
  matrix products  155 us (21%)
  between operations  19.3 us (3%)
  blocking collectives  13.4 us (2%)
    all_gather x1, waiting for transfers between devices, on_device(): whole_sum = jnp.sum(lax.all_gather(partial_value, 'col'), axis=0)  140 us
    another operation x13, other arithmetic, solve_rows(): factor_low = lax.linalg.cholesky(gram)  68.7 us
    dot_general x24, matrix products, one_step(): jnp.dot(select, result.reshape(group_size, block_edge * rank_width), prec...  55 us
    reshape x12, local copies, waits for them, and re-layouts, one_step(): tensor_group.reshape(group_size, block_edge, block_edge, block_edge)  52.3 us
    dot_general x12, matrix products, one_step(): jnp.einsum('bijk,bikr->bjr', tensor_group.reshape(group_size, block_edge,...  48.5 us
    convert_element_type x12, other arithmetic, one_step(): (left_blk[:, :, None, :] * tail_blk[:, None, :, :]).astype(jnp.bfloat16)  46.2 us
    gather x24, local copies, waits for them, and re-layouts, one_step(): left_blk = left_table[left_idx].astype(jnp.float32)  42.9 us
    psum x1, waiting for transfers between devices, on_device(): gram_first = lax.psum(jnp.dot(a_whole.T, a_whole, precision=highest), 'grp')  40.6 us
  transfers between devices with their start and end apart: 5, of which 3 were waited for; matrix products, arithmetic and copies ran while one was open for 36% of the time, Pallas kernels for 0%

profile of v1, /device:TPU:0, one launch (start us, length us, event | category | flops | bytes accessed | tf_op | source)
XLA Modules:
  0.0 732.6 jit_solution(10082113581654510926)
XLA Ops:
  14.8 13.4 %all_gather.10 = bf16[512,256]{1,0:T(8,128)(2,1)S(1)} all-gather(bf16[128,256]{1,0:T(8,128)(2,1)S(1)} %convert_element_type.56), channel_id=1, replica_groups=mesh['grp'=4,'col'=32] {'grp'}, dimensions={0}, use_global_device_ids=true | all-gather | bytes 327680 | tf_op jit(solution)/shard_map/all_gather | solution.py:91
  28.2 9.8 %all-gather.3.cloned.1.call-done = bf16[2048,256]{1,0:T(8,128)(2,1)} async-done(((bf16[512,256]{1,0:T(8,128)(2,1)}), bf16[2048,256]{1,0:T(8,128)(2,1)}) %all-gather.3.cloned.1.call-update) | async-done | bytes 1048592 | tf_op jit(solution)/shard_map/all_gather | solution.py:90
  38.0 141.1 %while.26 = (s32[]{:T(128)}, f32[64,8192]{1,0:T(8,128)S(1)}, s32[12,16]{1,0:T(8,128)S(1)}, f32[12,16]{1,0:T(8,128)S(1)}, bf16[12,16,32,1024]{3,2,1,0:T(8,128)(2,...) while((s32[]{:T(128)}, f32[64,8192]{1,0:T(8,128)S(1)}, ...), condition=%wide.region_1.0_spmd.clone, body=%wide.region_0.0_spmd.clone.sunk | while | flops 378802272 | bytes 27796492 | solution.py:75
  40.5 3.9 multiply_convert_fusion.5
  44.3 2.7 fusion.109
  52.2 3.9 multiply_convert_fusion.5
  64.0 3.9 multiply_convert_fusion.5
  67.9 2.7 fusion.109
  75.8 3.9 multiply_convert_fusion.5
  79.6 2.7 fusion.109
  87.5 3.9 multiply_convert_fusion.5
  99.3 3.9 multiply_convert_fusion.5
  103.2 2.7 fusion.109
  111.1 3.9 multiply_convert_fusion.5
  114.9 2.7 fusion.109
  122.8 3.9 multiply_convert_fusion.5
  126.7 2.7 fusion.109
  134.6 3.9 multiply_convert_fusion.5
  138.4 2.7 fusion.109
  146.4 3.9 multiply_convert_fusion.5
  150.2 2.7 fusion.109
  158.1 3.9 multiply_convert_fusion.5
  162.0 2.7 fusion.109
  169.9 3.9 multiply_convert_fusion.5
  173.8 2.7 fusion.109
  182.2 11.7 %custom-call.29 = f32[128,128]{1,0:T(8,128)S(1)} custom-call(f32[128,128]{1,0:T(8,128)S(1)} %slice.101), custom_call_target="Cholesky" | custom-call | tf_op jit(solution)/shard_map/cholesky/custom-call.2 | solution.py:10
  194.0 9.8 %custom-call.30 = f32[1,128,128]{1,2,0:T(8,128)S(1)} custom-call(f32[1,128,128]{2,1,0:T(8,128)S(1)} %get-tuple-element.264), custom_call_target="InvertDiagBlocksLowerTriangular" | custom-call | tf_op jit(solution)/shard_map/cholesky/custom-call.7 | solution.py:10
  204.5 11.7 %custom-call.31 = f32[128,128]{1,0:T(8,128)S(1)} custom-call(f32[128,128]{1,0:T(8,128)S(1)} %convolution_subtract_fusion.5), custom_call_target="Cholesky" | custom-call | tf_op jit(solution)/shard_map/cholesky/custom-call.3 | solution.py:10
  218.4 4.1 while.24
  222.5 19.7 %custom-call.20 = f32[2,128,128]{1,2,0:T(8,128)S(1)} custom-call(f32[2,128,128]{2,1,0:T(8,128)S(1)} %get-tuple-element.116), custom_call_target="InvertDiagBlocksLowerTriangular" | custom-call | tf_op jit(solution)/shard_map/triangular_solve | solution.py:11
  242.2 140.4 %all-gather.5.cloned.1.call-done = f32[32,2048,256]{2,1,0:T(8,128)} async-done(((f32[1,2048,256]{2,1,0:T(8,128)}), f32[32,2048,256]{2,1,0:T(8,128)}) %all-gather.5.cloned.1.call-update) | async-done | bytes 67108880 | tf_op jit(solution)/shard_map/all_gather | solution.py:100
  382.7 21.2 %reduce_sum.9 = f32[2048,256]{1,0:T(8,128)S(1)} reduce(f32[32,2048,256]{2,1,0:T(8,128)} %all-gather.5.cloned.1.call-done, f32[]{:T(128)} %constant.108.clone.1), dimensions={0}, to_apply=%region_2.3 | reduce | flops 16252928 | bytes 69206016 | tf_op jit(solution)/shard_map/reduce_sum | solution.py:100
  409.9 4.2 fusion.33
  414.1 40.6 %all-reduce.5.cloned.1.call-done = f32[256,256]{0,1:T(8,128)} async-done(((f32[256,256]{0,1:T(8,128)}), f32[256,256]{0,1:T(8,128)}) %all-reduce.5.cloned.1.call-update) | async-done | bytes 262160 | tf_op jit(solution)/shard_map/psum | solution.py:102
  459.9 195.1 %while.27 = (s32[]{:T(128)}, f32[64,8192]{1,0:T(8,128)S(1)}, s32[12,16]{1,0:T(8,128)}, f32[12,16]{1,0:T(8,128)}, bf16[12,16,32,1024]{3,2,1,0:T(8,128)(2,1)}, /*i...) while((s32[]{:T(128)}, f32[64,8192]{1,0:T(8,128)S(1)}, ...), condition=%wide.region_11.13_spmd.clone, body=%wide.region_10.12_spmd.clone.sunk | while | flops 378802272 | bytes 15213583 | solution.py:75
  461.4 4.4 reshape.341
  468.2 4.0 fusion.116
  477.6 4.4 reshape.341
  484.5 4.0 fusion.116
  493.8 4.4 reshape.341
  500.7 4.0 fusion.116
  510.1 4.4 reshape.341
  517.0 4.0 fusion.116
  526.3 4.4 reshape.341
  533.2 4.0 fusion.116
  542.6 4.4 reshape.341
  549.4 4.0 fusion.116
  558.8 4.4 reshape.341
  565.7 4.0 fusion.116
  575.1 4.4 reshape.341
  581.9 4.0 fusion.116
  591.3 4.4 reshape.341
  598.2 4.0 fusion.116
  607.6 4.4 reshape.341
  614.4 4.0 fusion.116
  623.8 4.4 reshape.341
  630.7 4.0 fusion.116
  640.0 4.4 reshape.341
  646.9 4.0 fusion.116
  659.1 11.7 %custom-call.32 = f32[128,128]{1,0:T(8,128)S(1)} custom-call(f32[128,128]{1,0:T(8,128)S(1)} %slice.104), custom_call_target="Cholesky" | custom-call | tf_op jit(solution)/shard_map/cholesky/custom-call.2 | solution.py:10
  670.9 9.8 %custom-call.33 = f32[1,128,128]{1,2,0:T(8,128)S(1)} custom-call(f32[1,128,128]{2,1,0:T(8,128)S(1)} %get-tuple-element.260), custom_call_target="InvertDiagBlocksLowerTriangular" | custom-call | tf_op jit(solution)/shard_map/cholesky/custom-call.7 | solution.py:10
  681.4 11.7 %custom-call.34 = f32[128,128]{1,0:T(8,128)S(1)} custom-call(f32[128,128]{1,0:T(8,128)S(1)} %convolution_subtract_fusion.4), custom_call_target="Cholesky" | custom-call | tf_op jit(solution)/shard_map/cholesky/custom-call.3 | solution.py:10
  695.9 4.0 while.25
  699.9 19.9 %custom-call.21 = f32[2,128,128]{1,2,0:T(8,128)S(1)} custom-call(f32[2,128,128]{2,1,0:T(8,128)S(1)} %get-tuple-element.124), custom_call_target="InvertDiagBlocksLowerTriangular" | custom-call | tf_op jit(solution)/shard_map/triangular_solve | solution.py:11
  (400 shorter events, 200.8 us)
Async XLA Ops:
  8.0 4.1 copy-start.5
  8.0 5.9 copy-start.8
  8.0 5.9 copy-start.12
  8.0 6.6 copy-start.13
  8.0 6.7 copy-start.14
  8.0 29.9 %all-gather.3.cloned.1.call-start = ((), (), s32[]{:S(2)}) async-start(), calls=%async_computation.1 | async-start | bytes 1310720 | tf_op jit(solution)/shard_map/all_gather | solution.py:90
  9.9 171.0 %all-reduce.7.cloned.1.call-start = ((), (), s32[]{:S(2)}) async-start(), calls=%async_computation.5 | async-start | bytes 1048576 | tf_op jit(solution)/shard_map/psum | solution.py:82
  13.8 368.8 %all-gather.5.cloned.1.call-start = ((), (), s32[]{:S(2)}) async-start(), calls=%async_computation.2 | async-start | bytes 69206016 | tf_op jit(solution)/shard_map/all_gather | solution.py:100
  179.1 1.5 copy-start.10
  179.2 1.5 copy-start.11
  180.7 274.1 %all-reduce.5.cloned.1.call-start = ((), (), s32[]{:S(2)}) async-start(), calls=%async_computation.3 | async-start | bytes 524288 | tf_op jit(solution)/shard_map/psum | solution.py:102
  222.5 160.1 %copy-start.6 = (f32[256,256]{1,0:T(8,128)}, f32[256,256]{1,0:T(8,128)S(1)}, u32[]{:S(2)}) copy-start(f32[256,256]{1,0:T(8,128)S(1)} %get-tuple-element.554) | copy-start | bytes 786436
  222.5 160.1 %copy-start.15 = (s32[2,2]{1,0:T(2,128)}, s32[2,2]{1,0:T(2,128)S(1)}, u32[]{:S(2)}) copy-start(s32[2,2]{1,0:T(2,128)S(1)} %get-tuple-element.572) | copy-start | bytes 52
  403.9 1.0 copy-start.7
  407.9 49.5 %copy-start = (f32[2048,128]{1,0:T(8,128)}, f32[2048,128]{1,0:T(8,128)S(1)}, u32[]{:S(2)}) copy-start(f32[2048,128]{1,0:T(8,128)S(1)} %fusion.48) | copy-start | bytes 3145732
  409.9 4.2 copy-start.2
  414.0 305.8 %reduce-scatter.2.cloned.1.call-start = ((), (), s32[]{:S(2)}) async-start(), calls=%async_computation.4 | async-start | bytes 2621440 | tf_op jit(solution)/shard_map/reduce_scatter | solution.py:111
  656.5 1.2 copy-start.1
  656.5 1.5 copy-start.3
  656.5 2.2 copy-start.4
  656.5 2.2 copy-start.9
  658.9 37.0 %copy-start.16 = (s32[2,2]{1,0:T(2,128)S(1)}, s32[2,2]{1,0:T(2,128)}, u32[]{:S(2)}) copy-start(s32[2,2]{1,0:T(2,128)} %copy-done.15) | copy-start | bytes 52
Sparse Core Ops, SparseCore 0:
  11.1 26.8 all-gather.2
  180.8 201.7 all-gather.4
  414.2 40.5 all-reduce.4
  656.6 30.1 reduce-scatter.1
Sparse Core Ops, SparseCore 1:
  15.4 148.4 all-reduce.6
